TPU v7x, 32 devices: a whole 2x2x4 slice. The times are simulated.
32 devices in a mesh: ctx: 8 (over y, x, core), hs: 4 (over z).
Axes of the slice: x: 2, y: 2, z: 4, core: 2. Of those that a mesh axis runs over, the one named last changes fastest.
Arguments:
- queries: bfloat16 [4096, 4096], P(('ctx', 'hs')), may hold values from -6 to 6
- key_matrix: bfloat16 [4096, 512], P(('ctx', 'hs')), may hold values from -6 to 6
- value_matrix: bfloat16 [4096, 512], P(('ctx', 'hs')), may hold values from -6 to 6
- output_gradient: bfloat16 [4096, 4096], P(('ctx', 'hs')), may hold values from -6 to 6
- doc_lengths: int32 [8], replicated, may hold values from 1 to 2048, 4096 in all
- windows: int32 [32], replicated, may hold values from 32 to 256, as said below
Outputs:
- query_grad: bfloat16 [4096, 4096], P(('ctx', 'hs'))
- key_grad: bfloat16 [4096, 512], P(('ctx', 'hs'))
Inputs may be any that keep to these rules, and one draw needn't show every extreme that they name: `doc_lengths`: the document lengths sum to 4096; the longest is exactly 2048. `windows`: A head's window counts the positions it may see, its own included; some head's window is exactly 256.
All inputs are finite; a program needn't handle non-finite values.
Results may differ from a plain program's by a relative error of at most 0.012.
Values may be sent and summed in bfloat16 or wider, within the bound.
A program may use at most 64 MiB of HBM per device.

v0:
```python
import functools
import math

import jax
import jax.numpy as jnp
from jax import lax
from jax.experimental import pallas as pl
from jax.experimental.pallas import tpu as pltpu
from jax.sharding import PartitionSpec as P

QUERY_HEADS = 32
KEY_VALUE_HEADS = 4
HEAD_SIZE = 128
WINDOW_LIMIT = 256

NEG_FILL = -1e30
MESH = pl.DeviceIdType.MESH
PAIR = 2
HALO = 2
DIRECT = 1


def attention_kernel(
    ctx_count,
    hs_count,
    rows,
    doc_ref,
    win_ref,
    q_hbm,
    k_hbm,
    v_hbm,
    do_hbm,
    dq_ref,
    dk_ref,
    q_ref,
    do_ref,
    kx_ref,
    vx_ref,
    own_ref,
    ds_ref,
    qs_ref,
    out_buf,
    in_buf,
    local_sem,
    fs_sem,
    fr_sem,
    bs_sem,
    br_sem,
):
    group = QUERY_HEADS // KEY_VALUE_HEADS
    group_cols = group * HEAD_SIZE
    c, z = lax.axis_index("ctx"), lax.axis_index("hs")
    place = c * hs_count + z
    total = ctx_count * hs_count
    edge = HALO * rows
    ext = edge + rows

    has_next = z <= hs_count - 2
    has_skip = (z >= hs_count - 2) & (c < ctx_count - 1)
    has_prev = z >= 1
    has_back = (z <= 1) & (c > 0)
    passes_on = has_prev & has_next
    passes_back = (z == 1) & (c > 0)

    def at(step):
        index = place + step
        return (lax.div(index, hs_count), lax.rem(index, hs_count))

    def cols(g):
        return pl.ds(pl.multiple_of(g * HEAD_SIZE, HEAD_SIZE), HEAD_SIZE)

    def wide(g):
        return pl.ds(pl.multiple_of(g * group_cols, group_cols), group_cols)

    def loads(g):
        return (
            pltpu.make_async_copy(q_hbm.at[:, wide(g)], q_ref.at[:, wide(g)], local_sem.at[0, g]),
            pltpu.make_async_copy(
                do_hbm.at[:, wide(g)], do_ref.at[:, wide(g)], local_sem.at[1, g]
            ),
            pltpu.make_async_copy(
                k_hbm.at[:, cols(g)], kx_ref.at[pl.ds(edge, rows), cols(g)], local_sem.at[2, g]
            ),
            pltpu.make_async_copy(
                v_hbm.at[:, cols(g)], vx_ref.at[pl.ds(edge, rows), cols(g)], local_sem.at[3, g]
            ),
        )

    def block_rows(slot):
        return pl.ds(edge - slot * rows, rows)

    def forward(kind, g, source, slot, step):
        pairs = ((k_hbm, kx_ref), (v_hbm, vx_ref))
        return tuple(
            pltpu.make_async_remote_copy(
                src_ref=src.at[:, cols(g)] if source == 0 else dst.at[block_rows(source), cols(g)],
                dst_ref=dst.at[block_rows(slot), cols(g)],
                send_sem=fs_sem.at[i, kind, g],
                recv_sem=fr_sem.at[i, slot - 1, g],
                device_id=at(step),
                device_id_type=MESH,
            )
            for i, (src, dst) in enumerate(pairs)
        )

    own_next = lambda g: forward(0, g, 0, 1, 1)
    own_skip = lambda g: forward(1, g, 0, 2, 2)
    pass_on = lambda g: forward(2, g, 1, 2, 1)
    pass_back = lambda g: forward(3, g, 2, 1, -1)

    def backward(g, part, target, step):
        return pltpu.make_async_remote_copy(
            src_ref=out_buf.at[part, :, cols(g)],
            dst_ref=in_buf.at[target, :, cols(g)],
            send_sem=bs_sem.at[part, g],
            recv_sem=br_sem.at[target, g],
            device_id=at(step),
            device_id_type=MESH,
        )

    def start(copies):
        for copy in copies:
            copy.start()

    def received(copies):
        for copy in copies:
            copy.wait_recv()

    def sent(copies):
        for copy in copies:
            copy.wait_send()

    barrier = pltpu.get_barrier_semaphore()
    neighbours = (
        (place + 1 < total, 1),
        (place + 2 < total, 2),
        (place >= 1, -1),
        (place >= 2, -2),
    )
    for there, step in neighbours:

        @pl.when(there)
        def _():
            pl.semaphore_signal(barrier, inc=1, device_id=at(step), device_id_type=MESH)

    @pl.loop(0, KEY_VALUE_HEADS)
    def _(g):
        start(loads(g))

    for slot in range(1, HALO + 1):

        @pl.when(place < slot)
        def _():
            kx_ref[block_rows(slot), :] = jnp.zeros((rows, kx_ref.shape[1]), kx_ref.dtype)
            vx_ref[block_rows(slot), :] = jnp.zeros((rows, vx_ref.shape[1]), vx_ref.dtype)

    peers = sum(there.astype(jnp.int32) for there, _ in neighbours)
    pl.semaphore_wait(barrier, peers)

    def sends_next(g):
        return has_next | ((g < DIRECT) & (place + 1 < total))

    def sends_skip(g):
        return has_skip | ((g < DIRECT) & (place + 2 < total))

    @pl.loop(0, KEY_VALUE_HEADS)
    def _(g):
        @pl.when(sends_next(g))
        def _():
            start(own_next(g))

        @pl.when(sends_skip(g))
        def _():
            start(own_skip(g))

    def arrive(g):
        @pl.when(place >= 1)
        def _():
            received(own_next(g))

        @pl.when(passes_on & (g >= DIRECT))
        def _():
            start(pass_on(g))

        @pl.when(passes_back & (g >= DIRECT))
        def _():
            received(own_skip(g))
            start(pass_back(g))

    base = place * rows
    query_off = lax.broadcasted_iota(jnp.int32, (1, rows), 1)
    query_pos = query_off + base

    def doc_step(n, carry):
        start, begin = carry
        begin = jnp.where(query_pos >= start, start, begin)
        return start + doc_ref[n], begin

    _, begin = lax.fori_loop(
        0, doc_ref.shape[0], doc_step, (jnp.int32(0), jnp.zeros((1, rows), jnp.int32))
    )
    begin_rel = begin - base + edge

    scale = 1.0 / math.sqrt(HEAD_SIZE)
    scale2 = scale * math.log2(math.e)
    key_off = lax.broadcasted_iota(jnp.int32, (rows, PAIR * rows), 0)
    causal = key_off <= jnp.concatenate([query_off] * PAIR, axis=1)

    def take(total_ref, source, g):
        backward(g, 0, source, -1).wait_recv()
        total_ref[:, cols(g)] = (
            total_ref[:, cols(g)].astype(jnp.float32) + in_buf[source, :, cols(g)].astype(jnp.float32)
        ).astype(total_ref.dtype)

    def combine(g):
        @pl.when(passes_on)
        def _():
            take(out_buf.at[0], 2, g)
            backward(g, 0, 0, -1).start()

        @pl.when(passes_back)
        def _():
            take(out_buf.at[1], 3, g)
            backward(g, 1, 0, -2).start()

    @pl.loop(0, KEY_VALUE_HEADS)
    def _(g):
        for copy in loads(g):
            copy.wait()

        @pl.when(g < DIRECT)
        def _():
            arrive(g)

        @pl.when((place >= 2) & jnp.logical_not(passes_back & (g >= DIRECT)))
        def _():
            received(own_skip(g))

        keys = kx_ref[:, cols(g)]
        values = vx_ref[:, cols(g)]
        keys_t = keys.astype(jnp.float32).T.astype(jnp.bfloat16)
        for pair in range(group // PAIR):
            heads = [g * group + pair * PAIR + n for n in range(PAIR)]
            queries = jnp.concatenate([q_ref[:, cols(h)] for h in heads], axis=0)
            gradout = jnp.concatenate([do_ref[:, cols(h)] for h in heads], axis=0)
            lowest = jnp.concatenate(
                [jnp.maximum(begin_rel, query_off + (edge + 1) - win_ref[h]) for h in heads],
                axis=1,
            )
            dims = (((1,), (1,)), ((), ()))
            tiles = []
            row_max = None
            for t in range(ext // rows):
                tile = lax.dot_general(
                    keys[t * rows : (t + 1) * rows], queries, dims, preferred_element_type=jnp.float32
                )
                allowed = key_off >= lowest - t * rows
                if t == ext // rows - 1:
                    allowed = allowed & causal
                tile = jnp.where(allowed, tile, NEG_FILL)
                top = jnp.max(tile, axis=0, keepdims=True)
                row_max = top if row_max is None else jnp.maximum(row_max, top)
                tiles.append(tile)
            total_sum, total_dot = 0.0, 0.0
            parts = []
            for t, tile in enumerate(tiles):
                shifted = jnp.exp2((tile - row_max) * scale2)
                dprob = lax.dot_general(
                    values[t * rows : (t + 1) * rows], gradout, dims, preferred_element_type=jnp.float32
                )
                total_sum = total_sum + jnp.sum(shifted, axis=0, keepdims=True)
                total_dot = total_dot + jnp.sum(shifted * dprob, axis=0, keepdims=True)
                parts.append((shifted, dprob))
            inverse = 1.0 / total_sum
            delta = total_dot * inverse
            factor = inverse * scale
            dscore = jnp.concatenate(
                [((s * factor) * (d - delta)).astype(jnp.bfloat16) for s, d in parts], axis=0
            )
            ds_ref[:, pair * PAIR * rows : (pair + 1) * PAIR * rows] = dscore
            qs_ref[pair * PAIR * rows : (pair + 1) * PAIR * rows, :] = queries

        dkx = lax.dot_general(
            ds_ref[...], qs_ref[...], (((1,), (0,)), ((), ())), preferred_element_type=jnp.float32
        )
        own_ref[:, cols(g)] = dkx[edge:]
        out_buf[0, :, cols(g)] = dkx[rows:edge].astype(jnp.bfloat16)
        out_buf[1, :, cols(g)] = dkx[:rows].astype(jnp.bfloat16)

        straight = g >= KEY_VALUE_HEADS - DIRECT

        @pl.when(straight & (place >= 1))
        def _():
            backward(g, 0, 0, -1).start()

        @pl.when(straight & (place >= 2))
        def _():
            backward(g, 1, 1, -2).start()

        @pl.when(jnp.logical_not(straight) & (z >= 2))
        def _():
            backward(g, 1, 2, -1).start()

        @pl.when(jnp.logical_not(straight) & (z == 0) & (c > 0))
        def _():
            backward(g, 0, 3, 1).start()
            backward(g, 1, 1, -2).start()

        @pl.when(jnp.logical_not(straight) & (z == hs_count - 1))
        def _():
            backward(g, 0, 0, -1).start()

        for pair in range(group // PAIR):
            dq_t = lax.dot_general(
                keys_t,
                ds_ref[:, pair * PAIR * rows : (pair + 1) * PAIR * rows],
                (((1,), (0,)), ((), ())),
                preferred_element_type=jnp.float32,
            )
            for n in range(PAIR):
                h = g * group + pair * PAIR + n
                dq_ref[:, cols(h)] = dq_t[:, n * rows : (n + 1) * rows].T.astype(jnp.bfloat16)

        @pl.when(g >= 1)
        def _():
            combine(g - 1)

        @pl.when(g == DIRECT - 1)
        def _():
            pl.loop(DIRECT, KEY_VALUE_HEADS)(arrive)


    @pl.loop(0, KEY_VALUE_HEADS)
    def _(g):
        straight = g >= KEY_VALUE_HEADS - DIRECT

        @pl.when(has_next | has_skip)
        def _():
            take(own_ref, 0, g)

        @pl.when(((z == hs_count - 2) & has_skip) | (straight & (place + 2 < total)))
        def _():
            take(own_ref, 1, g)

        dk_ref[:, cols(g)] = own_ref[:, cols(g)].astype(jnp.bfloat16)

    @pl.loop(0, KEY_VALUE_HEADS)
    def _(g):
        for there, copies in (
            (sends_next(g), own_next),
            (sends_skip(g), own_skip),
            (passes_on & (g >= DIRECT), pass_on),
            (passes_back & (g >= DIRECT), pass_back),
        ):

            @pl.when(there)
            def _():
                sent(copies(g))

        @pl.when(place >= 1)
        def _():
            backward(g, 0, 0, -1).wait_send()

        @pl.when(place >= 2)
        def _():
            backward(g, 1, 0, -1).wait_send()


def shards(queries, key_matrix, value_matrix, output_gradient, doc_lengths, windows):
    rows = queries.shape[0]
    ctx_count, hs_count = lax.axis_size("ctx"), lax.axis_size("hs")
    if HALO * rows < WINDOW_LIMIT - 1 or hs_count < 3:
        raise ValueError("unsupported shape")
    groups = KEY_VALUE_HEADS
    ext = (HALO + 1) * rows
    kv_cols = key_matrix.shape[1]
    any_spec = pl.BlockSpec(memory_space=pltpu.HBM)
    smem_spec = pl.BlockSpec(memory_space=pltpu.SMEM)
    return pl.pallas_call(
        functools.partial(attention_kernel, ctx_count, hs_count, rows),
        out_shape=(
            pltpu.VMEM(queries.shape, jnp.bfloat16),
            pltpu.VMEM(key_matrix.shape, jnp.bfloat16),
        ),
        in_specs=[smem_spec, smem_spec, any_spec, any_spec, any_spec, any_spec],
        out_specs=(pl.BlockSpec(memory_space=pltpu.VMEM), pl.BlockSpec(memory_space=pltpu.VMEM)),
        scratch_shapes=[
            pltpu.VMEM(queries.shape, jnp.bfloat16),
            pltpu.VMEM(queries.shape, jnp.bfloat16),
            pltpu.VMEM((ext, kv_cols), jnp.bfloat16),
            pltpu.VMEM((ext, kv_cols), jnp.bfloat16),
            pltpu.VMEM((rows, kv_cols), jnp.float32),
            pltpu.VMEM((ext, QUERY_HEADS // KEY_VALUE_HEADS * rows), jnp.bfloat16),
            pltpu.VMEM((QUERY_HEADS // KEY_VALUE_HEADS * rows, HEAD_SIZE), jnp.bfloat16),
            pltpu.VMEM((2, rows, kv_cols), jnp.bfloat16),
            pltpu.VMEM((4, rows, kv_cols), jnp.bfloat16),
            pltpu.SemaphoreType.DMA((4, groups)),
            pltpu.SemaphoreType.DMA((2, 4, groups)),
            pltpu.SemaphoreType.DMA((2, HALO, groups)),
            pltpu.SemaphoreType.DMA((2, groups)),
            pltpu.SemaphoreType.DMA((4, groups)),
        ],
        compiler_params=pltpu.CompilerParams(collective_id=0, has_side_effects=True),
    )(doc_lengths, windows, queries, key_matrix, value_matrix, output_gradient)


def solution(mesh):
    spec = P(("ctx", "hs"), None)
    return jax.shard_map(
        shards,
        mesh=mesh,
        in_specs=(spec, spec, spec, spec, P(), P()),
        out_specs=(spec, spec),
        check_vma=False,
    )
```

profile of v0, /device:TPU:25, one launch (start us, length us, event | category | flops | bytes accessed | tf_op | source)
XLA Modules:
  0.0 35.4 jit_solution(16604289668046457997)
XLA Ops:
  0.6 33.1 %shard_map.77 = (bf16[128,4096]{1,0:T(8,128)(2,1)S(1)}, bf16[128,512]{1,0:T(8,128)(2,1)S(1)}) custom-call(s32[8]{0:T(128)} %doc_ref.1, s32[32]{0:T(128)} %win_ref.1, bf16[128,4096]{1,0:T(8,128)(2,1)} %q_hbm.1, bf16[128,512]{1,0:T(8,128)(2,1)} %k_hbm.1, bf16[128,512]{1,0:T(8,128)(2,1)} %v_hbm.1, bf16[128,4096]{1,0:T(8,128)(2,1)} %do_hbm.1), custom_call_target="tpu_custom_call" | custom-call | tf_op jit(solution)/shard_map/pallas_call | solution.py:379
  33.8 1.0 %copy.10 = bf16[128,4096]{1,0:T(8,128)(2,1)} copy(bf16[128,4096]{1,0:T(8,128)(2,1)S(1)} %get-tuple-element.2) | data formatting | bytes 2097152
  34.7 0.7 %copy.11 = bf16[128,512]{1,0:T(8,128)(2,1)} copy(bf16[128,512]{1,0:T(8,128)(2,1)S(1)} %get-tuple-element.3) | data formatting | bytes 262144
where the time goes:
time: 35.6 us; the launch traced here: 35.4 us
  Pallas kernels  33.1 us (93%)
  local copies, waits for them, and re-layouts  1.63 us (5%)
  between operations  0.64 us (2%)
    pallas_call x1, Pallas kernels, shards(): pl.pallas_call(functools.partial(attention_kernel, ctx_count, hs_count, r...  33.1 us
    unnamed x2, local copies, waits for them, and re-layouts  1.63 us

commit v1 on v0

--- a/solution.py
+++ b/solution.py
@@ -17,7 +17,7 @@
 MESH = pl.DeviceIdType.MESH
 PAIR = 2
 HALO = 2
-DIRECT = 1
+AHEAD = 2
 
 
 def attention_kernel(
@@ -55,12 +55,9 @@
     edge = HALO * rows
     ext = edge + rows
 
-    has_next = z <= hs_count - 2
-    has_skip = (z >= hs_count - 2) & (c < ctx_count - 1)
-    has_prev = z >= 1
-    has_back = (z <= 1) & (c > 0)
-    passes_on = has_prev & has_next
-    passes_back = (z == 1) & (c > 0)
+    after = place + 1 < total
+    sends_on = ((z >= 2) & (z <= hs_count - 2)) | ((z == 0) & (c > 0))
+    joins = (z >= 3) | ((z == 1) & (c > 0))
 
     def at(step):
         index = place + step
@@ -89,7 +86,7 @@
     def block_rows(slot):
         return pl.ds(edge - slot * rows, rows)
 
-    def forward(kind, g, source, slot, step):
+    def forward(kind, g, source, slot):
         pairs = ((k_hbm, kx_ref), (v_hbm, vx_ref))
         return tuple(
             pltpu.make_async_remote_copy(
@@ -97,16 +94,14 @@
                 dst_ref=dst.at[block_rows(slot), cols(g)],
                 send_sem=fs_sem.at[i, kind, g],
                 recv_sem=fr_sem.at[i, slot - 1, g],
-                device_id=at(step),
+                device_id=at(1),
                 device_id_type=MESH,
             )
             for i, (src, dst) in enumerate(pairs)
         )
 
-    own_next = lambda g: forward(0, g, 0, 1, 1)
-    own_skip = lambda g: forward(1, g, 0, 2, 2)
-    pass_on = lambda g: forward(2, g, 1, 2, 1)
-    pass_back = lambda g: forward(3, g, 2, 1, -1)
+    own_next = lambda g: forward(0, g, 0, 1)
+    pass_on = lambda g: forward(1, g, 1, 2)
 
     def backward(g, part, target, step):
         return pltpu.make_async_remote_copy(
@@ -131,17 +126,10 @@
             copy.wait_send()
 
     barrier = pltpu.get_barrier_semaphore()
-    neighbours = (
-        (place + 1 < total, 1),
-        (place + 2 < total, 2),
-        (place >= 1, -1),
-        (place >= 2, -2),
-    )
-    for there, step in neighbours:
-
-        @pl.when(there)
-        def _():
-            pl.semaphore_signal(barrier, inc=1, device_id=at(step), device_id_type=MESH)
+
+    @pl.when(place >= 1)
+    def _():
+        pl.semaphore_signal(barrier, inc=1, device_id=at(-1), device_id_type=MESH)
 
     @pl.loop(0, KEY_VALUE_HEADS)
     def _(g):
@@ -154,38 +142,31 @@
             kx_ref[block_rows(slot), :] = jnp.zeros((rows, kx_ref.shape[1]), kx_ref.dtype)
             vx_ref[block_rows(slot), :] = jnp.zeros((rows, vx_ref.shape[1]), vx_ref.dtype)
 
-    peers = sum(there.astype(jnp.int32) for there, _ in neighbours)
-    pl.semaphore_wait(barrier, peers)
-
-    def sends_next(g):
-        return has_next | ((g < DIRECT) & (place + 1 < total))
-
-    def sends_skip(g):
-        return has_skip | ((g < DIRECT) & (place + 2 < total))
-
-    @pl.loop(0, KEY_VALUE_HEADS)
-    def _(g):
-        @pl.when(sends_next(g))
+    @pl.when(after)
+    def _():
+        pl.semaphore_wait(barrier, 1)
+
+    def send(g):
+        @pl.when(after & (g < KEY_VALUE_HEADS))
         def _():
             start(own_next(g))
 
-        @pl.when(sends_skip(g))
-        def _():
-            start(own_skip(g))
-
-    def arrive(g):
+    ahead = jnp.where(z == 0, KEY_VALUE_HEADS, AHEAD)
+    pl.loop(0, ahead)(send)
+
+    def relay(g):
         @pl.when(place >= 1)
         def _():
             received(own_next(g))
 
-        @pl.when(passes_on & (g >= DIRECT))
+        @pl.when(after & (place >= 1))
         def _():
             start(pass_on(g))
 
-        @pl.when(passes_back & (g >= DIRECT))
-        def _():
-            received(own_skip(g))
-            start(pass_back(g))
+        send(g + ahead)
+
+    first = jnp.where(z == 1, KEY_VALUE_HEADS, 1)
+    pl.loop(0, first)(relay)
 
     base = place * rows
     query_off = lax.broadcasted_iota(jnp.int32, (1, rows), 1)
@@ -212,29 +193,25 @@
             total_ref[:, cols(g)].astype(jnp.float32) + in_buf[source, :, cols(g)].astype(jnp.float32)
         ).astype(total_ref.dtype)
 
-    def combine(g):
-        @pl.when(passes_on)
-        def _():
-            take(out_buf.at[0], 2, g)
-            backward(g, 0, 0, -1).start()
-
-        @pl.when(passes_back)
-        def _():
-            take(out_buf.at[1], 3, g)
-            backward(g, 1, 0, -2).start()
+    def join(g):
+        take(out_buf.at[1], 2, g)
+
+        @pl.when(place >= 2)
+        def _():
+            backward(g, 1, 1, -2).start()
 
     @pl.loop(0, KEY_VALUE_HEADS)
     def _(g):
         for copy in loads(g):
             copy.wait()
 
-        @pl.when(g < DIRECT)
-        def _():
-            arrive(g)
-
-        @pl.when((place >= 2) & jnp.logical_not(passes_back & (g >= DIRECT)))
-        def _():
-            received(own_skip(g))
+        @pl.when((z != 1) & (g + 1 < KEY_VALUE_HEADS))
+        def _():
+            relay(g + 1)
+
+        @pl.when(place >= 2)
+        def _():
+            received(pass_on(g))
 
         keys = kx_ref[:, cols(g)]
         values = vx_ref[:, cols(g)]
@@ -287,28 +264,21 @@
         out_buf[0, :, cols(g)] = dkx[rows:edge].astype(jnp.bfloat16)
         out_buf[1, :, cols(g)] = dkx[:rows].astype(jnp.bfloat16)
 
-        straight = g >= KEY_VALUE_HEADS - DIRECT
-
-        @pl.when(straight & (place >= 1))
+        @pl.when(sends_on)
+        def _():
+            backward(g, 0, 2, 1).start()
+
+        @pl.when(jnp.logical_not(sends_on) & (place >= 1))
         def _():
             backward(g, 0, 0, -1).start()
 
-        @pl.when(straight & (place >= 2))
+        @pl.when(jnp.logical_not(joins) & (place >= 2))
         def _():
             backward(g, 1, 1, -2).start()
 
-        @pl.when(jnp.logical_not(straight) & (z >= 2))
-        def _():
-            backward(g, 1, 2, -1).start()
-
-        @pl.when(jnp.logical_not(straight) & (z == 0) & (c > 0))
-        def _():
-            backward(g, 0, 3, 1).start()
-            backward(g, 1, 1, -2).start()
-
-        @pl.when(jnp.logical_not(straight) & (z == hs_count - 1))
-        def _():
-            backward(g, 0, 0, -1).start()
+        @pl.when(joins & (g >= 1))
+        def _():
+            join(g - 1)
 
         for pair in range(group // PAIR):
             dq_t = lax.dot_general(
@@ -321,24 +291,17 @@
                 h = g * group + pair * PAIR + n
                 dq_ref[:, cols(h)] = dq_t[:, n * rows : (n + 1) * rows].T.astype(jnp.bfloat16)
 
-        @pl.when(g >= 1)
-        def _():
-            combine(g - 1)
-
-        @pl.when(g == DIRECT - 1)
-        def _():
-            pl.loop(DIRECT, KEY_VALUE_HEADS)(arrive)
-
+    @pl.when(joins)
+    def _():
+        join(KEY_VALUE_HEADS - 1)
 
     @pl.loop(0, KEY_VALUE_HEADS)
     def _(g):
-        straight = g >= KEY_VALUE_HEADS - DIRECT
-
-        @pl.when(has_next | has_skip)
+        @pl.when((z == 0) | (z == hs_count - 2))
         def _():
             take(own_ref, 0, g)
 
-        @pl.when(((z == hs_count - 2) & has_skip) | (straight & (place + 2 < total)))
+        @pl.when(place + 2 < total)
         def _():
             take(own_ref, 1, g)
 
@@ -346,12 +309,7 @@
 
     @pl.loop(0, KEY_VALUE_HEADS)
     def _(g):
-        for there, copies in (
-            (sends_next(g), own_next),
-            (sends_skip(g), own_skip),
-            (passes_on & (g >= DIRECT), pass_on),
-            (passes_back & (g >= DIRECT), pass_back),
-        ):
+        for there, copies in ((after, own_next), (after & (place >= 1), pass_on)):
 
             @pl.when(there)
             def _():
@@ -363,7 +321,7 @@
 
         @pl.when(place >= 2)
         def _():
-            backward(g, 1, 0, -1).wait_send()
+            backward(g, 1, 1, -2).wait_send()
 
 
 def shards(queries, key_matrix, value_matrix, output_gradient, doc_lengths, windows):
@@ -393,12 +351,12 @@
             pltpu.VMEM((ext, QUERY_HEADS // KEY_VALUE_HEADS * rows), jnp.bfloat16),
             pltpu.VMEM((QUERY_HEADS // KEY_VALUE_HEADS * rows, HEAD_SIZE), jnp.bfloat16),
             pltpu.VMEM((2, rows, kv_cols), jnp.bfloat16),
-            pltpu.VMEM((4, rows, kv_cols), jnp.bfloat16),
+            pltpu.VMEM((3, rows, kv_cols), jnp.bfloat16),
             pltpu.SemaphoreType.DMA((4, groups)),
-            pltpu.SemaphoreType.DMA((2, 4, groups)),
+            pltpu.SemaphoreType.DMA((2, 2, groups)),
             pltpu.SemaphoreType.DMA((2, HALO, groups)),
             pltpu.SemaphoreType.DMA((2, groups)),
-            pltpu.SemaphoreType.DMA((4, groups)),
+            pltpu.SemaphoreType.DMA((3, groups)),
         ],
         compiler_params=pltpu.CompilerParams(collective_id=0, has_side_effects=True),
     )(doc_lengths, windows, queries, key_matrix, value_matrix, output_gradient)

time: 35.6 us -> 28.9 us (0.81)
  the two profiles are of different devices: /device:TPU:25 before, /device:TPU:27 now
where the time goes in v1:
time: 28.9 us; the launch traced here: 28.7 us
  Pallas kernels  26.5 us (92%)
  local copies, waits for them, and re-layouts  1.63 us (6%)
  between operations  0.64 us (2%)
    pallas_call x1, Pallas kernels, shards(): pl.pallas_call(functools.partial(attention_kernel, ctx_count, hs_count, r...  26.5 us
    unnamed x2, local copies, waits for them, and re-layouts  1.63 us

profile of v1, /device:TPU:27, one launch (start us, length us, event | category | flops | bytes accessed | tf_op | source)
XLA Modules:
  0.0 28.7 jit_solution(6972280447507658445)
XLA Ops:
  0.6 26.5 %shard_map.77 = (bf16[128,4096]{1,0:T(8,128)(2,1)S(1)}, bf16[128,512]{1,0:T(8,128)(2,1)S(1)}) custom-call(s32[8]{0:T(128)} %doc_ref.1, s32[32]{0:T(128)} %win_ref.1, bf16[128,4096]{1,0:T(8,128)(2,1)} %q_hbm.1, bf16[128,512]{1,0:T(8,128)(2,1)} %k_hbm.1, bf16[128,512]{1,0:T(8,128)(2,1)} %v_hbm.1, bf16[128,4096]{1,0:T(8,128)(2,1)} %do_hbm.1), custom_call_target="tpu_custom_call" | custom-call | tf_op jit(solution)/shard_map/pallas_call | solution.py:337
  27.1 1.0 %copy.10 = bf16[128,4096]{1,0:T(8,128)(2,1)} copy(bf16[128,4096]{1,0:T(8,128)(2,1)S(1)} %get-tuple-element.2) | data formatting | bytes 2097152
  28.1 0.7 %copy.11 = bf16[128,512]{1,0:T(8,128)(2,1)} copy(bf16[128,512]{1,0:T(8,128)(2,1)S(1)} %get-tuple-element.3) | data formatting | bytes 262144

commit v2 on v1

--- a/solution.py
+++ b/solution.py
@@ -18,20 +18,24 @@
 PAIR = 2
 HALO = 2
 AHEAD = 2
+DIRECT = 1
+WRAP = 2
 
 
 def attention_kernel(
     ctx_count,
     hs_count,
     rows,
-    doc_ref,
-    win_ref,
+    doc_hbm,
+    win_hbm,
     q_hbm,
     k_hbm,
     v_hbm,
     do_hbm,
     dq_ref,
     dk_ref,
+    doc_ref,
+    win_ref,
     q_ref,
     do_ref,
     kx_ref,
@@ -41,6 +45,7 @@
     qs_ref,
     out_buf,
     in_buf,
+    table_sem,
     local_sem,
     fs_sem,
     fr_sem,
@@ -69,12 +74,16 @@
     def wide(g):
         return pl.ds(pl.multiple_of(g * group_cols, group_cols), group_cols)
 
-    def loads(g):
+    def rows_of(g):
         return (
             pltpu.make_async_copy(q_hbm.at[:, wide(g)], q_ref.at[:, wide(g)], local_sem.at[0, g]),
             pltpu.make_async_copy(
                 do_hbm.at[:, wide(g)], do_ref.at[:, wide(g)], local_sem.at[1, g]
             ),
+        )
+
+    def keys_of(g):
+        return (
             pltpu.make_async_copy(
                 k_hbm.at[:, cols(g)], kx_ref.at[pl.ds(edge, rows), cols(g)], local_sem.at[2, g]
             ),
@@ -131,9 +140,10 @@
     def _():
         pl.semaphore_signal(barrier, inc=1, device_id=at(-1), device_id_type=MESH)
 
-    @pl.loop(0, KEY_VALUE_HEADS)
-    def _(g):
-        start(loads(g))
+    tables = (
+        pltpu.make_async_copy(doc_hbm, doc_ref, table_sem.at[0]),
+        pltpu.make_async_copy(win_hbm, win_ref, table_sem.at[1]),
+    )
 
     for slot in range(1, HALO + 1):
 
@@ -153,6 +163,11 @@
 
     ahead = jnp.where(z == 0, KEY_VALUE_HEADS, AHEAD)
     pl.loop(0, ahead)(send)
+    start(tables)
+
+    @pl.loop(0, KEY_VALUE_HEADS)
+    def _(g):
+        start(keys_of(g) + rows_of(g))
 
     def relay(g):
         @pl.when(place >= 1)
@@ -167,6 +182,9 @@
 
     first = jnp.where(z == 1, KEY_VALUE_HEADS, 1)
     pl.loop(0, first)(relay)
+
+    for copy in tables:
+        copy.wait()
 
     base = place * rows
     query_off = lax.broadcasted_iota(jnp.int32, (1, rows), 1)
@@ -186,6 +204,8 @@
     scale2 = scale * math.log2(math.e)
     key_off = lax.broadcasted_iota(jnp.int32, (rows, PAIR * rows), 0)
     causal = key_off <= jnp.concatenate([query_off] * PAIR, axis=1)
+    own_or_far = jnp.where(causal, key_off + edge, key_off)
+    own_part = jnp.where(causal, 1.0, 0.0).astype(jnp.bfloat16)
 
     def take(total_ref, source, g):
         backward(g, 0, source, -1).wait_recv()
@@ -193,6 +213,9 @@
             total_ref[:, cols(g)].astype(jnp.float32) + in_buf[source, :, cols(g)].astype(jnp.float32)
         ).astype(total_ref.dtype)
 
+    def straight(g):
+        return g >= KEY_VALUE_HEADS - jnp.where(z <= 1, WRAP, DIRECT)
+
     def join(g):
         take(out_buf.at[1], 2, g)
 
@@ -202,7 +225,7 @@
 
     @pl.loop(0, KEY_VALUE_HEADS)
     def _(g):
-        for copy in loads(g):
+        for copy in keys_of(g) + rows_of(g):
             copy.wait()
 
         @pl.when((z != 1) & (g + 1 < KEY_VALUE_HEADS))
@@ -224,37 +247,37 @@
                 [jnp.maximum(begin_rel, query_off + (edge + 1) - win_ref[h]) for h in heads],
                 axis=1,
             )
-            dims = (((1,), (1,)), ((), ()))
-            tiles = []
-            row_max = None
-            for t in range(ext // rows):
-                tile = lax.dot_general(
-                    keys[t * rows : (t + 1) * rows], queries, dims, preferred_element_type=jnp.float32
+            def against(block):
+                far, near, own = (
+                    lax.dot_general(
+                        block[t * rows : (t + 1) * rows],
+                        other,
+                        (((1,), (1,)), ((), ())),
+                        preferred_element_type=jnp.float32,
+                    )
+                    for t in range(HALO + 1)
                 )
-                allowed = key_off >= lowest - t * rows
-                if t == ext // rows - 1:
-                    allowed = allowed & causal
-                tile = jnp.where(allowed, tile, NEG_FILL)
-                top = jnp.max(tile, axis=0, keepdims=True)
-                row_max = top if row_max is None else jnp.maximum(row_max, top)
-                tiles.append(tile)
-            total_sum, total_dot = 0.0, 0.0
-            parts = []
-            for t, tile in enumerate(tiles):
-                shifted = jnp.exp2((tile - row_max) * scale2)
-                dprob = lax.dot_general(
-                    values[t * rows : (t + 1) * rows], gradout, dims, preferred_element_type=jnp.float32
-                )
-                total_sum = total_sum + jnp.sum(shifted, axis=0, keepdims=True)
-                total_dot = total_dot + jnp.sum(shifted * dprob, axis=0, keepdims=True)
-                parts.append((shifted, dprob))
-            inverse = 1.0 / total_sum
-            delta = total_dot * inverse
+                return jnp.where(causal, own, far), near
+
+            other = queries
+            outer, inner = against(keys)
+            outer = jnp.where(own_or_far >= lowest, outer, NEG_FILL)
+            inner = jnp.where(key_off >= lowest - rows, inner, NEG_FILL)
+            row_max = jnp.max(jnp.maximum(outer, inner), axis=0, keepdims=True)
+            outer = jnp.exp2((outer - row_max) * scale2)
+            inner = jnp.exp2((inner - row_max) * scale2)
+            other = gradout
+            outer_d, inner_d = against(values)
+            inverse = 1.0 / jnp.sum(outer + inner, axis=0, keepdims=True)
+            delta = jnp.sum(outer * outer_d + inner * inner_d, axis=0, keepdims=True) * inverse
             factor = inverse * scale
-            dscore = jnp.concatenate(
-                [((s * factor) * (d - delta)).astype(jnp.bfloat16) for s, d in parts], axis=0
-            )
-            ds_ref[:, pair * PAIR * rows : (pair + 1) * PAIR * rows] = dscore
+            outer = ((outer * factor) * (outer_d - delta)).astype(jnp.bfloat16)
+            inner = ((inner * factor) * (inner_d - delta)).astype(jnp.bfloat16)
+            own = outer * own_part
+            lanes = slice(pair * PAIR * rows, (pair + 1) * PAIR * rows)
+            ds_ref[:rows, lanes] = outer - own
+            ds_ref[rows:edge, lanes] = inner
+            ds_ref[edge:, lanes] = own
             qs_ref[pair * PAIR * rows : (pair + 1) * PAIR * rows, :] = queries
 
         dkx = lax.dot_general(
@@ -264,19 +287,19 @@
         out_buf[0, :, cols(g)] = dkx[rows:edge].astype(jnp.bfloat16)
         out_buf[1, :, cols(g)] = dkx[:rows].astype(jnp.bfloat16)
 
-        @pl.when(sends_on)
+        @pl.when(sends_on & jnp.logical_not(straight(g)))
         def _():
             backward(g, 0, 2, 1).start()
 
-        @pl.when(jnp.logical_not(sends_on) & (place >= 1))
+        @pl.when((straight(g) | jnp.logical_not(sends_on)) & (place >= 1))
         def _():
             backward(g, 0, 0, -1).start()
 
-        @pl.when(jnp.logical_not(joins) & (place >= 2))
+        @pl.when((straight(g) | jnp.logical_not(joins)) & (place >= 2))
         def _():
             backward(g, 1, 1, -2).start()
 
-        @pl.when(joins & (g >= 1))
+        @pl.when(joins & (g >= 1) & jnp.logical_not(straight(g - 1)))
         def _():
             join(g - 1)
 
@@ -291,13 +314,9 @@
                 h = g * group + pair * PAIR + n
                 dq_ref[:, cols(h)] = dq_t[:, n * rows : (n + 1) * rows].T.astype(jnp.bfloat16)
 
-    @pl.when(joins)
-    def _():
-        join(KEY_VALUE_HEADS - 1)
-
     @pl.loop(0, KEY_VALUE_HEADS)
     def _(g):
-        @pl.when((z == 0) | (z == hs_count - 2))
+        @pl.when((z == 0) | (z == hs_count - 2) | ((g >= KEY_VALUE_HEADS - jnp.where(z == hs_count - 1, WRAP, DIRECT)) & after))
         def _():
             take(own_ref, 0, g)
 
@@ -324,25 +343,37 @@
             backward(g, 1, 1, -2).wait_send()
 
 
+def store_kernel(dq_ref, dk_ref, dq_hbm, dk_hbm, sem):
+    copies = (
+        pltpu.make_async_copy(dq_ref, dq_hbm, sem.at[0]),
+        pltpu.make_async_copy(dk_ref, dk_hbm, sem.at[1]),
+    )
+    for copy in copies:
+        copy.start()
+    for copy in copies:
+        copy.wait()
+
+
 def shards(queries, key_matrix, value_matrix, output_gradient, doc_lengths, windows):
     rows = queries.shape[0]
     ctx_count, hs_count = lax.axis_size("ctx"), lax.axis_size("hs")
-    if HALO * rows < WINDOW_LIMIT - 1 or hs_count < 3:
+    if HALO * rows < WINDOW_LIMIT or hs_count < 3:
         raise ValueError("unsupported shape")
     groups = KEY_VALUE_HEADS
     ext = (HALO + 1) * rows
     kv_cols = key_matrix.shape[1]
     any_spec = pl.BlockSpec(memory_space=pltpu.HBM)
-    smem_spec = pl.BlockSpec(memory_space=pltpu.SMEM)
-    return pl.pallas_call(
+    grads = pl.pallas_call(
         functools.partial(attention_kernel, ctx_count, hs_count, rows),
         out_shape=(
             pltpu.VMEM(queries.shape, jnp.bfloat16),
             pltpu.VMEM(key_matrix.shape, jnp.bfloat16),
         ),
-        in_specs=[smem_spec, smem_spec, any_spec, any_spec, any_spec, any_spec],
+        in_specs=[any_spec, any_spec, any_spec, any_spec, any_spec, any_spec],
         out_specs=(pl.BlockSpec(memory_space=pltpu.VMEM), pl.BlockSpec(memory_space=pltpu.VMEM)),
         scratch_shapes=[
+            pltpu.SMEM(doc_lengths.shape, jnp.int32),
+            pltpu.SMEM(windows.shape, jnp.int32),
             pltpu.VMEM(queries.shape, jnp.bfloat16),
             pltpu.VMEM(queries.shape, jnp.bfloat16),
             pltpu.VMEM((ext, kv_cols), jnp.bfloat16),
@@ -352,6 +383,7 @@
             pltpu.VMEM((QUERY_HEADS // KEY_VALUE_HEADS * rows, HEAD_SIZE), jnp.bfloat16),
             pltpu.VMEM((2, rows, kv_cols), jnp.bfloat16),
             pltpu.VMEM((3, rows, kv_cols), jnp.bfloat16),
+            pltpu.SemaphoreType.DMA((2,)),
             pltpu.SemaphoreType.DMA((4, groups)),
             pltpu.SemaphoreType.DMA((2, 2, groups)),
             pltpu.SemaphoreType.DMA((2, HALO, groups)),
@@ -360,6 +392,18 @@
         ],
         compiler_params=pltpu.CompilerParams(collective_id=0, has_side_effects=True),
     )(doc_lengths, windows, queries, key_matrix, value_matrix, output_gradient)
+    vmem_spec = pl.BlockSpec(memory_space=pltpu.VMEM)
+    return pl.pallas_call(
+        store_kernel,
+        out_shape=(
+            jax.ShapeDtypeStruct(queries.shape, jnp.bfloat16),
+            jax.ShapeDtypeStruct(key_matrix.shape, jnp.bfloat16),
+        ),
+        in_specs=[pl.BlockSpec(memory_space=pl.ANY)] * 2,
+        out_specs=(any_spec, any_spec),
+        scratch_shapes=[pltpu.SemaphoreType.DMA((2,))],
+        compiler_params=pltpu.CompilerParams(vmem_limit_bytes=2**20),
+    )(*grads)
 
 
 def solution(mesh):

time: 28.9 us -> 26.4 us (0.913)
  the two profiles are of different devices: /device:TPU:27 before, /device:TPU:0 now
where the time goes in v2:
time: 26.4 us; the launch traced here: 26.2 us
  Pallas kernels  25.6 us (97%)
  between operations  0.64 us (2%)
    pallas_call x1, Pallas kernels, shards(): pl.pallas_call(functools.partial(attention_kernel, ctx_count, hs_count, r...  24.6 us
    pallas_call x1, Pallas kernels, shards(): pl.pallas_call(store_kernel, out_shape=(jax.ShapeDtypeStruct(queries.shap...  1.02 us

profile of v2, /device:TPU:0, one launch (start us, length us, event | category | flops | bytes accessed | tf_op | source)
XLA Modules:
  0.0 26.2 jit_solution(12009849087638392006)
XLA Ops:
  0.6 24.6 %shard_map.77 = (bf16[128,4096]{1,0:T(8,128)(2,1)S(1)}, bf16[128,512]{1,0:T(8,128)(2,1)S(1)}) custom-call(s32[8]{0:T(128)} %doc_hbm.1, s32[32]{0:T(128)} %win_hbm.1, bf16[128,4096]{1,0:T(8,128)(2,1)} %q_hbm.1, bf16[128,512]{1,0:T(8,128)(2,1)} %k_hbm.1, bf16[128,512]{1,0:T(8,128)(2,1)} %v_hbm.1, bf16[128,4096]{1,0:T(8,128)(2,1)} %do_hbm.1), custom_call_target="tpu_custom_call" | custom-call | tf_op jit(solution)/shard_map/pallas_call | solution.py:366
  25.2 1.0 %shard_map.78 = (bf16[128,4096]{1,0:T(8,128)(2,1)}, bf16[128,512]{1,0:T(8,128)(2,1)}) custom-call(bf16[128,4096]{1,0:T(8,128)(2,1)S(1)} %get-tuple-element.4.dq_ref, bf16[128,512]{1,0:T(8,128)(2,1)S(1)} %get-tuple-element.5.dk_ref), custom_call_target="tpu_custom_call" | custom-call | tf_op jit(solution)/shard_map/pallas_call | solution.py:396

commit v3 on v2

--- a/solution.py
+++ b/solution.py
@@ -19,7 +19,6 @@
 HALO = 2
 AHEAD = 2
 DIRECT = 1
-WRAP = 2
 
 
 def attention_kernel(
@@ -61,6 +60,7 @@
     ext = edge + rows
 
     after = place + 1 < total
+    last = z == hs_count - 1
     sends_on = ((z >= 2) & (z <= hs_count - 2)) | ((z == 0) & (c > 0))
     joins = (z >= 3) | ((z == 1) & (c > 0))
 
@@ -180,7 +180,7 @@
 
         send(g + ahead)
 
-    first = jnp.where(z == 1, KEY_VALUE_HEADS, 1)
+    first = jnp.where(z == 1, KEY_VALUE_HEADS, jnp.where(last, 2, 1))
     pl.loop(0, first)(relay)
 
     for copy in tables:
@@ -213,8 +213,21 @@
             total_ref[:, cols(g)].astype(jnp.float32) + in_buf[source, :, cols(g)].astype(jnp.float32)
         ).astype(total_ref.dtype)
 
+    def turned_keys(g):
+        return kx_ref[:, cols(g)].astype(jnp.float32).T.astype(jnp.bfloat16)
+
+    def query_grads(g, keys_t, pair):
+        lanes = slice(pair * PAIR * rows, (pair + 1) * PAIR * rows)
+        dq_t = lax.dot_general(
+            keys_t, ds_ref[:, lanes], (((1,), (0,)), ((), ())), preferred_element_type=jnp.float32
+        )
+        for n in range(PAIR):
+            dq_ref[:, cols(g * group + pair * PAIR + n)] = (
+                dq_t[:, n * rows : (n + 1) * rows].T.astype(jnp.bfloat16)
+            )
+
     def straight(g):
-        return g >= KEY_VALUE_HEADS - jnp.where(z <= 1, WRAP, DIRECT)
+        return g >= KEY_VALUE_HEADS - DIRECT
 
     def join(g):
         take(out_buf.at[1], 2, g)
@@ -228,9 +241,9 @@
         for copy in keys_of(g) + rows_of(g):
             copy.wait()
 
-        @pl.when((z != 1) & (g + 1 < KEY_VALUE_HEADS))
-        def _():
-            relay(g + 1)
+        @pl.when(g + first < KEY_VALUE_HEADS)
+        def _():
+            relay(g + first)
 
         @pl.when(place >= 2)
         def _():
@@ -238,8 +251,10 @@
 
         keys = kx_ref[:, cols(g)]
         values = vx_ref[:, cols(g)]
-        keys_t = keys.astype(jnp.float32).T.astype(jnp.bfloat16)
+        before = lax.div(g * (KEY_VALUE_HEADS - 1), KEY_VALUE_HEADS)
+        keys_t = turned_keys(before)
         for pair in range(group // PAIR):
+            query_grads(before, keys_t, pair)
             heads = [g * group + pair * PAIR + n for n in range(PAIR)]
             queries = jnp.concatenate([q_ref[:, cols(h)] for h in heads], axis=0)
             gradout = jnp.concatenate([do_ref[:, cols(h)] for h in heads], axis=0)
@@ -303,28 +318,13 @@
         def _():
             join(g - 1)
 
-        for pair in range(group // PAIR):
-            dq_t = lax.dot_general(
-                keys_t,
-                ds_ref[:, pair * PAIR * rows : (pair + 1) * PAIR * rows],
-                (((1,), (0,)), ((), ())),
-                preferred_element_type=jnp.float32,
-            )
-            for n in range(PAIR):
-                h = g * group + pair * PAIR + n
-                dq_ref[:, cols(h)] = dq_t[:, n * rows : (n + 1) * rows].T.astype(jnp.bfloat16)
-
-    @pl.loop(0, KEY_VALUE_HEADS)
-    def _(g):
-        @pl.when((z == 0) | (z == hs_count - 2) | ((g >= KEY_VALUE_HEADS - jnp.where(z == hs_count - 1, WRAP, DIRECT)) & after))
-        def _():
-            take(own_ref, 0, g)
-
-        @pl.when(place + 2 < total)
-        def _():
-            take(own_ref, 1, g)
-
-        dk_ref[:, cols(g)] = own_ref[:, cols(g)].astype(jnp.bfloat16)
+    final_keys_t = turned_keys(KEY_VALUE_HEADS - 1)
+    for pair in range(group // PAIR):
+        query_grads(KEY_VALUE_HEADS - 1, final_keys_t, pair)
+
+    @pl.when(joins & jnp.logical_not(straight(KEY_VALUE_HEADS - 1)))
+    def _():
+        join(KEY_VALUE_HEADS - 1)
 
     @pl.loop(0, KEY_VALUE_HEADS)
     def _(g):
@@ -341,6 +341,18 @@
         @pl.when(place >= 2)
         def _():
             backward(g, 1, 1, -2).wait_send()
+
+    @pl.loop(0, KEY_VALUE_HEADS)
+    def _(g):
+        @pl.when((z == 0) | (z == hs_count - 2) | (straight(g) & after))
+        def _():
+            take(own_ref, 0, g)
+
+        @pl.when(place + 2 < total)
+        def _():
+            take(own_ref, 1, g)
+
+        dk_ref[:, cols(g)] = own_ref[:, cols(g)].astype(jnp.bfloat16)
 
 
 def store_kernel(dq_ref, dk_ref, dq_hbm, dk_hbm, sem):

time: 26.4 us -> 26.3 us (level)
  no operation moved by 1% of the time
where the time goes in v3:
time: 26.3 us; the launch traced here: 26.1 us
  Pallas kernels  25.5 us (97%)
  between operations  0.64 us (2%)
    pallas_call x1, Pallas kernels, shards(): pl.pallas_call(functools.partial(attention_kernel, ctx_count, hs_count, r...  24.5 us
    pallas_call x1, Pallas kernels, shards(): pl.pallas_call(store_kernel, out_shape=(jax.ShapeDtypeStruct(queries.shap...  1.02 us

profile of v3, /device:TPU:0, one launch (start us, length us, event | category | flops | bytes accessed | tf_op | source)
XLA Modules:
  0.0 26.1 jit_solution(5970453440983095848)
XLA Ops:
  0.6 24.5 %shard_map.77 = (bf16[128,4096]{1,0:T(8,128)(2,1)S(1)}, bf16[128,512]{1,0:T(8,128)(2,1)S(1)}) custom-call(s32[8]{0:T(128)} %doc_hbm.1, s32[32]{0:T(128)} %win_hbm.1, bf16[128,4096]{1,0:T(8,128)(2,1)} %q_hbm.1, bf16[128,512]{1,0:T(8,128)(2,1)} %k_hbm.1, bf16[128,512]{1,0:T(8,128)(2,1)} %v_hbm.1, bf16[128,4096]{1,0:T(8,128)(2,1)} %do_hbm.1), custom_call_target="tpu_custom_call" | custom-call | tf_op jit(solution)/shard_map/pallas_call | solution.py:378
  25.1 1.0 %shard_map.78 = (bf16[128,4096]{1,0:T(8,128)(2,1)}, bf16[128,512]{1,0:T(8,128)(2,1)}) custom-call(bf16[128,4096]{1,0:T(8,128)(2,1)S(1)} %get-tuple-element.4.dq_ref, bf16[128,512]{1,0:T(8,128)(2,1)S(1)} %get-tuple-element.5.dk_ref), custom_call_target="tpu_custom_call" | custom-call | tf_op jit(solution)/shard_map/pallas_call | solution.py:408

commit v4 on v3

--- a/solution.py
+++ b/solution.py
@@ -161,7 +161,7 @@
         def _():
             start(own_next(g))
 
-    ahead = jnp.where(z == 0, KEY_VALUE_HEADS, AHEAD)
+    ahead = jnp.where((z == 0) | (z == hs_count - 2), KEY_VALUE_HEADS, AHEAD)
     pl.loop(0, ahead)(send)
     start(tables)
 
@@ -180,7 +180,7 @@
 
         send(g + ahead)
 
-    first = jnp.where(z == 1, KEY_VALUE_HEADS, jnp.where(last, 2, 1))
+    first = jnp.where(z == 0, 2, jnp.where((z == 1) | last, KEY_VALUE_HEADS, 1))
     pl.loop(0, first)(relay)
 
     for copy in tables:

time: 26.3 us -> 26.3 us (level)
  no operation moved by 1% of the time
where the time goes in v4:
time: 26.3 us; the launch traced here: 26.1 us
  Pallas kernels  25.5 us (97%)
  between operations  0.64 us (2%)
    pallas_call x1, Pallas kernels, shards(): pl.pallas_call(functools.partial(attention_kernel, ctx_count, hs_count, r...  24.4 us
    pallas_call x1, Pallas kernels, shards(): pl.pallas_call(store_kernel, out_shape=(jax.ShapeDtypeStruct(queries.shap...  1.02 us

profile of v4, /device:TPU:0, one launch (start us, length us, event | category | flops | bytes accessed | tf_op | source)
XLA Modules:
  0.0 26.1 jit_solution(3177898120895126343)
XLA Ops:
  0.6 24.4 %shard_map.77 = (bf16[128,4096]{1,0:T(8,128)(2,1)S(1)}, bf16[128,512]{1,0:T(8,128)(2,1)S(1)}) custom-call(s32[8]{0:T(128)} %doc_hbm.1, s32[32]{0:T(128)} %win_hbm.1, bf16[128,4096]{1,0:T(8,128)(2,1)} %q_hbm.1, bf16[128,512]{1,0:T(8,128)(2,1)} %k_hbm.1, bf16[128,512]{1,0:T(8,128)(2,1)} %v_hbm.1, bf16[128,4096]{1,0:T(8,128)(2,1)} %do_hbm.1), custom_call_target="tpu_custom_call" | custom-call | tf_op jit(solution)/shard_map/pallas_call | solution.py:378
  25.1 1.0 %shard_map.78 = (bf16[128,4096]{1,0:T(8,128)(2,1)}, bf16[128,512]{1,0:T(8,128)(2,1)}) custom-call(bf16[128,4096]{1,0:T(8,128)(2,1)S(1)} %get-tuple-element.4.dq_ref, bf16[128,512]{1,0:T(8,128)(2,1)S(1)} %get-tuple-element.5.dk_ref), custom_call_target="tpu_custom_call" | custom-call | tf_op jit(solution)/shard_map/pallas_call | solution.py:408

commit v5 on v4

--- a/solution.py
+++ b/solution.py
@@ -344,15 +344,18 @@
 
     @pl.loop(0, KEY_VALUE_HEADS)
     def _(g):
-        @pl.when((z == 0) | (z == hs_count - 2) | (straight(g) & after))
-        def _():
-            take(own_ref, 0, g)
-
-        @pl.when(place + 2 < total)
-        def _():
-            take(own_ref, 1, g)
-
-        dk_ref[:, cols(g)] = own_ref[:, cols(g)].astype(jnp.bfloat16)
+        from_next = (z == 0) | (z == hs_count - 2) | (straight(g) & after)
+        total_grad = own_ref[:, cols(g)]
+        for source, there in ((0, from_next), (1, place + 2 < total)):
+
+            @pl.when(there)
+            def _():
+                backward(g, 0, source, -1).wait_recv()
+
+        for source, there in ((0, from_next), (1, place + 2 < total)):
+            part = in_buf[source, :, cols(g)].astype(jnp.float32)
+            total_grad = total_grad + jnp.where(there, part, 0.0)
+        dk_ref[:, cols(g)] = total_grad.astype(jnp.bfloat16)
 
 
 def store_kernel(dq_ref, dk_ref, dq_hbm, dk_hbm, sem):

time: 26.3 us -> 26.2 us (level)
  no operation moved by 1% of the time
where the time goes in v5:
time: 26.2 us; the launch traced here: 26.1 us
  Pallas kernels  25.5 us (97%)
  between operations  0.64 us (2%)
    pallas_call x1, Pallas kernels, shards(): pl.pallas_call(functools.partial(attention_kernel, ctx_count, hs_count, r...  24.4 us
    pallas_call x1, Pallas kernels, shards(): pl.pallas_call(store_kernel, out_shape=(jax.ShapeDtypeStruct(queries.shap...  1.02 us

profile of v5, /device:TPU:0, one launch (start us, length us, event | category | flops | bytes accessed | tf_op | source)
XLA Modules:
  0.0 26.1 jit_solution(10817350912066674191)
XLA Ops:
  0.6 24.4 %shard_map.77 = (bf16[128,4096]{1,0:T(8,128)(2,1)S(1)}, bf16[128,512]{1,0:T(8,128)(2,1)S(1)}) custom-call(s32[8]{0:T(128)} %doc_hbm.1, s32[32]{0:T(128)} %win_hbm.1, bf16[128,4096]{1,0:T(8,128)(2,1)} %q_hbm.1, bf16[128,512]{1,0:T(8,128)(2,1)} %k_hbm.1, bf16[128,512]{1,0:T(8,128)(2,1)} %v_hbm.1, bf16[128,4096]{1,0:T(8,128)(2,1)} %do_hbm.1), custom_call_target="tpu_custom_call" | custom-call | tf_op jit(solution)/shard_map/pallas_call | solution.py:381
  25.1 1.0 %shard_map.78 = (bf16[128,4096]{1,0:T(8,128)(2,1)}, bf16[128,512]{1,0:T(8,128)(2,1)}) custom-call(bf16[128,4096]{1,0:T(8,128)(2,1)S(1)} %get-tuple-element.4.dq_ref, bf16[128,512]{1,0:T(8,128)(2,1)S(1)} %get-tuple-element.5.dk_ref), custom_call_target="tpu_custom_call" | custom-call | tf_op jit(solution)/shard_map/pallas_call | solution.py:411

commit v6 on v4

--- a/solution.py
+++ b/solution.py
@@ -180,7 +180,7 @@
 
         send(g + ahead)
 
-    first = jnp.where(z == 0, 2, jnp.where((z == 1) | last, KEY_VALUE_HEADS, 1))
+    first = jnp.where(z == 0, 2, jnp.where((z == 1) | last, KEY_VALUE_HEADS, 2))
     pl.loop(0, first)(relay)
 
     for copy in tables:

time: 26.3 us -> 26.3 us (level)
  no operation moved by 1% of the time
where the time goes in v6:
time: 26.3 us; the launch traced here: 26.1 us
  Pallas kernels  25.5 us (97%)
  between operations  0.64 us (2%)
    pallas_call x1, Pallas kernels, shards(): pl.pallas_call(functools.partial(attention_kernel, ctx_count, hs_count, r...  24.4 us
    pallas_call x1, Pallas kernels, shards(): pl.pallas_call(store_kernel, out_shape=(jax.ShapeDtypeStruct(queries.shap...  1.02 us

profile of v6, /device:TPU:0, one launch (start us, length us, event | category | flops | bytes accessed | tf_op | source)
XLA Modules:
  0.0 26.1 jit_solution(16066882928069076106)
XLA Ops:
  0.6 24.4 %shard_map.77 = (bf16[128,4096]{1,0:T(8,128)(2,1)S(1)}, bf16[128,512]{1,0:T(8,128)(2,1)S(1)}) custom-call(s32[8]{0:T(128)} %doc_hbm.1, s32[32]{0:T(128)} %win_hbm.1, bf16[128,4096]{1,0:T(8,128)(2,1)} %q_hbm.1, bf16[128,512]{1,0:T(8,128)(2,1)} %k_hbm.1, bf16[128,512]{1,0:T(8,128)(2,1)} %v_hbm.1, bf16[128,4096]{1,0:T(8,128)(2,1)} %do_hbm.1), custom_call_target="tpu_custom_call" | custom-call | tf_op jit(solution)/shard_map/pallas_call | solution.py:378
  25.1 1.0 %shard_map.78 = (bf16[128,4096]{1,0:T(8,128)(2,1)}, bf16[128,512]{1,0:T(8,128)(2,1)}) custom-call(bf16[128,4096]{1,0:T(8,128)(2,1)S(1)} %get-tuple-element.4.dq_ref, bf16[128,512]{1,0:T(8,128)(2,1)S(1)} %get-tuple-element.5.dk_ref), custom_call_target="tpu_custom_call" | custom-call | tf_op jit(solution)/shard_map/pallas_call | solution.py:408
